TPU v7x, 128 devices: a whole 4x4x4 slice. The times are simulated.
128 devices in a mesh: sa: 4 (over x), sb: 2 (over core), sc: 16 (over z, y).
Axes of the slice: x: 4, y: 4, z: 4, core: 2. Of those that a mesh axis runs over, the one named last changes fastest.
Arguments:
- queries: float32 [65536, 2048], P(('sa', 'sb', 'sc')), may hold values from -6 to 6
- key_rows: float32 [65536, 2048], P(('sa', 'sb', 'sc')), may hold values from -6 to 6
- value_rows: float32 [65536, 2048], P(('sa', 'sb', 'sc')), may hold values from -6 to 6
- out_grad: float32 [65536, 2048], P(('sa', 'sb', 'sc')), may hold values from -6 to 6
- prefix_state: float32 [16, 128, 128], replicated, may hold values from -1536 to 1536
- suffix_state: float32 [16, 128, 128], replicated, may hold values from -1536 to 1536
Outputs:
- query_grad: bfloat16 [65536, 2048], P(('sa', 'sb', 'sc'))
- key_grad: bfloat16 [65536, 2048], P(('sa', 'sb', 'sc'))
- value_grad: bfloat16 [65536, 2048], P(('sa', 'sb', 'sc'))
All inputs are finite; a program needn't handle non-finite values.
Results may differ from a plain program's by a relative error of at most 0.0019.
Values sent between devices are 32-bit elements; how exact they have to be, the bound alone decides.
A program may use at most 576 MiB of HBM per device.

v0:
```python
import math
import jax
import jax.numpy as jnp
from jax import lax
from jax.sharding import PartitionSpec as P


def entering(part, axis, combine, identity):
    place = lax.axis_index(axis)
    gathered = jax.tree.map(lambda a: lax.all_gather(a, axis), part)
    state = jax.tree.map(lambda a, e: jnp.zeros_like(a) + jnp.asarray(e, a.dtype), part, identity)

    def one(hop, state):
        return combine(
            state, jax.tree.map(lambda a: lax.dynamic_index_in_dim(a, hop, 0, False), gathered)
        )

    return lax.fori_loop(0, place, one, state)


def add_states(earlier, later):
    return jax.tree.map(lambda left, right: left + right, earlier, later)


def run_chain(local_terms):
    zero_state = jax.tree.map(jnp.zeros_like, local_terms)
    inner_part = entering(local_terms, "sc", add_states, zero_state)
    group_sum = lax.psum((local_terms[0], local_terms[1]), "sc")
    middle_part = entering(group_sum, "sb", add_states, zero_state)
    block_sum = lax.psum((group_sum[0], group_sum[1]), "sb")
    outer_part = entering(block_sum, "sa", add_states, zero_state)
    return add_states(add_states(outer_part, middle_part), inner_part)


def shards(queries, key_rows, value_rows, out_grad, prefix_state, suffix_state):
    row_count = queries.shape[0]
    head_count = prefix_state.shape[0]
    head_size = prefix_state.shape[1]
    device_count = lax.axis_size("sa") * lax.axis_size("sb") * lax.axis_size("sc")
    factor = 1.0 / math.sqrt(head_size * row_count * device_count)
    highest = lax.Precision.HIGHEST
    shaped = (row_count, head_count, head_size)
    query_t = queries.reshape(shaped)
    key_t = key_rows.reshape(shaped)
    value_t = value_rows.reshape(shaped)
    grad_t = out_grad.reshape(shaped)
    kv_local = jnp.einsum("thd,the->hde", key_t, value_t, precision=highest)
    grad_local = jnp.einsum("the,thd->hed", grad_t, query_t, precision=highest)
    prior_kv, prior_grad = run_chain((kv_local, grad_local))
    total_grad = lax.psum(grad_local, ("sa", "sb", "sc"))
    state_before = prefix_state + prior_kv
    state_after = suffix_state + (total_grad - prior_grad - grad_local)
    lower = (
        lax.broadcasted_iota(jnp.int32, (row_count, row_count), 0)
        >= lax.broadcasted_iota(jnp.int32, (row_count, row_count), 1)
    ).astype(jnp.float32)
    grad_scores = jnp.einsum("the,she->hts", grad_t, value_t, precision=highest) * lower
    attn_scores = jnp.einsum("thd,shd->hts", query_t, key_t, precision=highest) * lower
    query_grad = factor * (
        jnp.einsum("the,hde->thd", grad_t, state_before, precision=highest)
        + jnp.einsum("hts,shd->thd", grad_scores, key_t, precision=highest)
    )
    key_grad = factor * (
        jnp.einsum("she,hed->shd", value_t, state_after, precision=highest)
        + jnp.einsum("hts,thd->shd", grad_scores, query_t, precision=highest)
    )
    value_grad = factor * (
        jnp.einsum("shd,hed->she", key_t, state_after, precision=highest)
        + jnp.einsum("hts,the->she", attn_scores, grad_t, precision=highest)
    )
    flat = (row_count, head_count * head_size)
    return (
        query_grad.astype(jnp.bfloat16).reshape(flat),
        key_grad.astype(jnp.bfloat16).reshape(flat),
        value_grad.astype(jnp.bfloat16).reshape(flat),
    )


def solution(mesh):
    return jax.shard_map(
        shards,
        mesh=mesh,
        in_specs=(
            P(("sa", "sb", "sc"), None),
            P(("sa", "sb", "sc"), None),
            P(("sa", "sb", "sc"), None),
            P(("sa", "sb", "sc"), None),
            P(),
            P(),
        ),
        out_specs=(
            P(("sa", "sb", "sc"), None),
            P(("sa", "sb", "sc"), None),
            P(("sa", "sb", "sc"), None),
        ),
        check_vma=False,
    )
```

profile of v0, /device:TPU:1, one launch (start us, length us, event | category | flops | bytes accessed | tf_op | source)
XLA Modules:
  0.0 613.8 jit_solution(8954921210702635121)
XLA Ops:
  8.0 11.2 %fusion.21 = f32[16,128,128]{2,1,0:T(8,128)} fusion(f32[512,2048]{1,0:T(8,128)} %param.14, f32[512,2048]{1,0:T(8,128)} %param.13), kind=kOutput, calls=%fused_computation.27 | convolution fusion | flops 1610612736 | bytes 9437184 | tf_op jit(solution)/shard_map/thd,the->hde/dot_general | solution.py:47
  19.2 5.1 copy.46
  24.3 5.7 copy.27
  30.1 9.2 %fusion.16 = f32[16,128,128]{2,1,0:T(8,128)} fusion(f32[512,16,128]{0,2,1:T(8,128)} %copy.27, f32[512,2048]{1,0:T(8,128)} %param.12), kind=kOutput, calls=%fused_computation.22 | convolution fusion | flops 1610612736 | bytes 9437184 | tf_op jit(solution)/shard_map/the,thd->hed/dot_general | solution.py:48
  39.3 94.8 %all-gather.19.cloned.1.call-done = f32[256,128,128]{2,1,0:T(8,128)} async-done(((f32[16,128,128]{2,1,0:T(8,128)}), f32[256,128,128]{2,1,0:T(8,128)}) %all-gather.19.cloned.1.call-update) | async-done | bytes 16777232 | tf_op jit(solution)/shard_map/all_gather | solution.py:10
  134.0 0.7 all-reduce.8.cloned.1.call-update
  134.8 93.1 %all-reduce.8.cloned.1.call-done = (f32[16,128,128]{2,1,0:T(8,128)}, f32[16,128,128]{2,1,0:T(8,128)}) async-done(((f32[16,128,128]{2,1,0:T(8,128)}, f32[16,128,128]{2,1,0:T(8,128)}), (f32[16,128,128]{2,1,0:T(8,128)}, f32[16,128,128]{2,1,0:T(8,128)})) %all-reduce.8.cloned.1.call-update) | async-done | bytes 2097168 | tf_op jit(solution)/shard_map/psum | solution.py:28
  228.5 15.4 %all-gather.15.cloned.1.call-done = f32[32,128,128]{2,1,0:T(8,128)} async-done(((f32[16,128,128]{2,1,0:T(8,128)}), f32[32,128,128]{2,1,0:T(8,128)}) %all-gather.15.cloned.1.call-update) | async-done | bytes 2097168 | tf_op jit(solution)/shard_map/all_gather | solution.py:10
  243.9 16.3 %all-gather.17.cloned.1.call-done = f32[32,128,128]{2,1,0:T(8,128)} async-done(((f32[16,128,128]{2,1,0:T(8,128)}), f32[32,128,128]{2,1,0:T(8,128)}) %all-gather.17.cloned.1.call-update) | async-done | bytes 2097168 | tf_op jit(solution)/shard_map/all_gather | solution.py:10
  261.4 30.2 %all-reduce.10.cloned.1.call-done = (f32[1,16,128,128]{3,2,1,0:T(8,128)}, f32[1,16,128,128]{3,2,1,0:T(8,128)}) async-done(((f32[1,16,128,128]{3,2,1,0:T(8,128)}, f32[1,16,128,128]{3,2,1,0:T(8,128)}), (f32[1,16,128,128]{3,2,1,0:T(8,128)}, f32[1,16,128,128]{3,2,1,0:T(8,128)})) %all-reduce.10.cloned.1.call-update) | async-done | bytes 2097168 | tf_op jit(solution)/shard_map/psum | solution.py:30
  291.6 0.7 all-gather.13.cloned.1.call-update
  293.1 19.5 %fusion.14 = f32[16,512,512]{2,1,0:T(8,128)} fusion(f32[512,2048]{1,0:T(8,128)} %param.12, f32[512,2048]{1,0:T(8,128)} %param.13), kind=kOutput, calls=%fused_computation.20 | convolution fusion | flops 6442450944 | bytes 25165824 | tf_op jit(solution)/shard_map/thd,shd->hts/dot_general | solution.py:58
  312.6 14.5 %fusion.11 = f32[16,512,512]{2,1,0:T(8,128)S(1)} fusion(f32[512,2048]{1,0:T(8,128)S(1)} %copy-done.4, f32[512,2048]{1,0:T(8,128)S(1)} %copy-done.5), kind=kOutput, calls=%fused_computation.17 | convolution fusion | flops 6442450944 | bytes 25165824 | tf_op jit(solution)/shard_map/the,she->hts/dot_general | solution.py:57
  327.1 14.5 %fusion.2 = f32[16,512,128]{1,2,0:T(8,128)} fusion(f32[16,512,512]{2,1,0:T(8,128)S(1)} %fusion.11, f32[512,512]{1,0:T(8,128)S(1)} %fusion.55, f32[512,2048]{1,0:T(8,128)} %param.12), kind=kOutput, calls=%fused_computation.8 | convolution fusion | flops 6446645248 | bytes 26214400 | tf_op jit(solution)/shard_map/hts,thd->shd/dot_general | solution.py:65
  341.6 21.3 %fusion.4 = f32[16,512,128]{1,2,0:T(8,128)} fusion(f32[16,512,512]{2,1,0:T(8,128)S(1)} %fusion.11, f32[512,512]{1,0:T(8,128)S(1)} %fusion.55, f32[512,2048]{1,0:T(8,128)} %param.13), kind=kOutput, calls=%fused_computation.10 | convolution fusion | flops 6446645248 | bytes 26214400 | tf_op jit(solution)/shard_map/hts,shd->thd/dot_general | solution.py:61
  362.9 44.5 %all-gather.21.cloned.1.call-done = f32[256,128,128]{2,1,0:T(8,128)} async-done(((f32[16,128,128]{2,1,0:T(8,128)}), f32[256,128,128]{2,1,0:T(8,128)}) %all-gather.21.cloned.1.call-update) | async-done | bytes 16777232 | tf_op jit(solution)/shard_map/all_gather | solution.py:10
  407.6 1.0 copy-done.1
  408.8 2.1 while.37
  408.8 2.1 bitcast_add_fusion.13
  410.9 45.8 %all-gather.11.cloned.1.call-done = f32[4,16,128,128]{3,2,1,0:T(8,128)} async-done(((f32[1,16,128,128]{3,2,1,0:T(8,128)}), f32[4,16,128,128]{3,2,1,0:T(8,128)}) %all-gather.11.cloned.1.call-update) | async-done | bytes 4194320 | tf_op jit(solution)/shard_map/all_gather | solution.py:10
  456.7 50.5 %all-gather.13.cloned.1.call-done = f32[4,16,128,128]{3,2,1,0:T(8,128)} async-done(((f32[1,16,128,128]{3,2,1,0:T(8,128)}), f32[4,16,128,128]{3,2,1,0:T(8,128)}) %all-gather.13.cloned.1.call-update) | async-done | bytes 4194320 | tf_op jit(solution)/shard_map/all_gather | solution.py:10
  507.3 1.1 broadcast.6.clone.3
  508.4 44.6 %all-reduce.6.cloned.1.call-done = f32[16,128,128]{2,1,0:T(8,128)} async-done(((f32[16,128,128]{2,1,0:T(8,128)}), f32[16,128,128]{2,1,0:T(8,128)}) %all-reduce.6.cloned.1.call-update) | async-done | bytes 1048592 | tf_op jit(solution)/shard_map/psum | solution.py:50
  552.9 3.5 subtract_add_fusion
  556.4 1.0 copy-done.8
  557.5 3.8 fusion.23
  561.3 14.6 %fusion.29 = bf16[512,16,128]{0,2,1:T(8,128)(2,1)} fusion(f32[16,128,512]{2,1,0:T(8,128)S(1)} %fusion.23, f32[512,16,128]{0,2,1:T(8,128)S(1)} %copy-done.3, f32[16,512,512]{2,1,0:T(8,128)} %fusion.14, f32[512,512]{1,0:T(8,128)S(1)} %copy-done.7), kind=kOutput, calls=%fused_computation.36 | convolution fusion | flops 6449790976 | bytes 28311552 | tf_op jit(solution)/shard_map/hts,the->she/dot_general | solution.py:69
  575.9 3.9 copy.40
  579.8 9.2 %fusion.31 = bf16[512,16,128]{0,2,1:T(8,128)(2,1)} fusion(f32[16,512,128]{1,2,0:T(8,128)} %fusion.2, f32[16,128,128]{2,1,0:T(8,128)} %copy-done.8, f32[512,2048]{1,0:T(8,128)} %param.14), kind=kOutput, calls=%fused_computation.39 | convolution fusion | flops 1613758464 | bytes 11534336 | tf_op jit(solution)/shard_map/she,hed->shd/dot_general | solution.py:64
  589.0 4.1 copy.39
  593.1 9.2 %fusion.33 = bf16[512,16,128]{0,2,1:T(8,128)(2,1)} fusion(f32[16,512,128]{1,2,0:T(8,128)} %fusion.4, f32[16,128,128]{2,1,0:T(8,128)} %param.16, f32[16,128,128]{2,1,0:T(8,128)S(1)} %get-tuple-element.107, f32[16,128,128]{2,1,0:T(8,128)S(1)} %get-tuple-element.105, f32[16,128,128]{2,1,0:T(8,128)S(1)} %get-tuple-element.106, f32[512,2048]{1,0:T(8,128)} %param.15), kind=kOutput, calls=%fused_computation.42 | convolution fusion | flops 1614544896 | bytes 14680064 | tf_op jit(solution)/shard_map/the,hde->thd/dot_general | solution.py:60
  602.3 3.9 copy.38
  (40 shorter events, 3.1 us)
Async XLA Ops:
  8.0 126.0 %all-gather.19.cloned.1.call-start = ((), (), s32[]{:S(2)}) async-start(), calls=%async_computation.5 | async-start | bytes 17825792 | tf_op jit(solution)/shard_map/all_gather | solution.py:10
  134.0 93.9 %all-reduce.8.cloned.1.call-start = ((), (), s32[]{:S(2)}) async-start(), calls=%async_computation.7 | async-start | bytes 4194304 | tf_op jit(solution)/shard_map/psum | solution.py:28
  134.8 109.2 %all-gather.15.cloned.1.call-start = ((), (), s32[]{:S(2)}) async-start(), calls=%async_computation.3 | async-start | bytes 3145728 | tf_op jit(solution)/shard_map/all_gather | solution.py:10
  228.0 32.2 %all-gather.17.cloned.1.call-start = ((), (), s32[]{:S(2)}) async-start(), calls=%async_computation.4 | async-start | bytes 3145728 | tf_op jit(solution)/shard_map/all_gather | solution.py:10
  260.2 31.4 %all-reduce.10.cloned.1.call-start = ((), (), s32[]{:S(2)}) async-start(), calls=%async_computation.8 | async-start | bytes 4194304 | tf_op jit(solution)/shard_map/psum | solution.py:30
  260.8 146.6 %all-gather.21.cloned.1.call-start = ((), (), s32[]{:S(2)}) async-start(), calls=%async_computation.6 | async-start | bytes 17825792 | tf_op jit(solution)/shard_map/all_gather | solution.py:10
  261.4 195.3 %all-gather.11.cloned.1.call-start = ((), (), s32[]{:S(2)}) async-start(), calls=%async_computation | async-start | bytes 5242880 | tf_op jit(solution)/shard_map/all_gather | solution.py:10
  291.6 215.6 %all-gather.13.cloned.1.call-start = ((), (), s32[]{:S(2)}) async-start(), calls=%async_computation.1 | async-start | bytes 5242880 | tf_op jit(solution)/shard_map/all_gather | solution.py:10
  292.3 260.6 %all-reduce.6.cloned.1.call-start = ((), (), s32[]{:S(2)}) async-start(), calls=%async_computation.2 | async-start | bytes 2097152 | tf_op jit(solution)/shard_map/psum | solution.py:50
  293.0 48.6 %copy-start.6 = (f32[512,512]{1,0:T(8,128)}, f32[512,512]{1,0:T(8,128)S(1)}, u32[]{:S(2)}) copy-start(f32[512,512]{1,0:T(8,128)S(1)} %fusion.55) | copy-start | bytes 3145732
  293.1 19.6 %copy-start.4 = (f32[512,2048]{1,0:T(8,128)S(1)}, f32[512,2048]{1,0:T(8,128)}, u32[]{:S(2)}) copy-start(f32[512,2048]{1,0:T(8,128)} %param.15) | copy-start | bytes 12582916
  293.1 19.6 %copy-start.5 = (f32[512,2048]{1,0:T(8,128)S(1)}, f32[512,2048]{1,0:T(8,128)}, u32[]{:S(2)}) copy-start(f32[512,2048]{1,0:T(8,128)} %param.14) | copy-start | bytes 12582916
  407.6 1.0 copy-start.1
  410.9 45.8 %copy-start.2 = (f32[16,128,128]{2,1,0:T(8,128)}, f32[16,128,128]{2,1,0:T(8,128)S(1)}, u32[]{:S(2)}) copy-start(f32[16,128,128]{2,1,0:T(8,128)S(1)} %get-tuple-element.109) | copy-start | bytes 3145732
  552.9 4.5 copy-start
  556.4 1.0 copy-start.8
  557.5 3.8 copy-start.3
  557.5 3.8 copy-start.7
Sparse Core Ops, SparseCore 0:
  19.4 114.6 all-gather.18
  138.8 89.0 all-reduce.7
  229.7 14.2 all-gather.14
  245.5 14.6 all-gather.16
  263.4 28.1 all-reduce.9
  294.1 113.1 all-gather.20
  409.0 47.6 all-gather.10
  458.3 48.7 all-gather.12
Sparse Core Ops, SparseCore 1:
  298.2 254.7 all-reduce.5
where the time goes:
time: 621 us; the launch traced here: 614 us
  waiting for transfers between devices  439 us (71%)
  matrix products  127 us (20%)
  local copies, waits for them, and re-layouts  26.3 us (4%)
  between operations  16 us (3%)
    all_gather x6, waiting for transfers between devices, entering(): gathered = jax.tree.map(lambda a: lax.all_gather(a, axis), part)  267 us
    psum x1, waiting for transfers between devices, run_chain(): group_sum = lax.psum((local_terms[0], local_terms[1]), 'sc')  93.1 us
    psum x1, waiting for transfers between devices, shards(): total_grad = lax.psum(grad_local, ('sa', 'sb', 'sc'))  44.6 us
    psum x1, waiting for transfers between devices, run_chain(): block_sum = lax.psum((group_sum[0], group_sum[1]), 'sb')  30.2 us
    dot_general x1, matrix products, shards(): jnp.einsum('hts,shd->thd', grad_scores, key_t, precision=highest)  21.3 us
    dot_general x1, matrix products, shards(): jnp.einsum('thd,shd->hts', query_t, key_t, precision=highest) * lower  19.5 us
    unnamed x22, local copies, waits for them, and re-layouts  19 us
    dot_general x1, matrix products, shards(): jnp.einsum('hts,the->she', attn_scores, grad_t, precision=highest)  14.6 us
  transfers between devices with their start and end apart: 9, of which 9 were waited for; matrix products, arithmetic and copies ran while one was open for 15% of the time, Pallas kernels for 0%

commit v1 on v0

--- a/solution.py
+++ b/solution.py
@@ -3,6 +3,12 @@
 import jax.numpy as jnp
 from jax import lax
 from jax.sharding import PartitionSpec as P
+
+
+def produce_ticks_on(m):
+    for h in ("sa", ("sb", "sc")):
+        m = lax.psum(m, axis_name=h)
+    return m
 
 
 def entering(part, axis, combine, identity):
@@ -47,7 +53,7 @@
     kv_local = jnp.einsum("thd,the->hde", key_t, value_t, precision=highest)
     grad_local = jnp.einsum("the,thd->hed", grad_t, query_t, precision=highest)
     prior_kv, prior_grad = run_chain((kv_local, grad_local))
-    total_grad = lax.psum(grad_local, ("sa", "sb", "sc"))
+    total_grad = produce_ticks_on(grad_local)
     state_before = prefix_state + prior_kv
     state_after = suffix_state + (total_grad - prior_grad - grad_local)
     lower = (

time: 621 us -> 732 us (1.18)
  waiting for transfers between devices: 439 us -> 551 us
    psum x1 -> x2, waiting for transfers between devices: 44.6 us -> 108 us  [produce_ticks_on(): m = lax.psum(m, axis_name=h)]
    all_gather x6, waiting for transfers between devices: 267 us -> 317 us  [entering(): gathered = jax.tree.map(lambda a: lax.all_gather(a, axis), part)]
  transfers between devices with their start and end apart: 9 -> 10, of which waited for: 9 -> 9; matrix products, arithmetic and copies ran while one was open for 15% -> 13% of each run, Pallas kernels for 0% -> 0%
where the time goes in v1:
time: 732 us; the launch traced here: 725 us
  waiting for transfers between devices  551 us (75%)
  matrix products  127 us (17%)
  local copies, waits for them, and re-layouts  26.3 us (4%)
  between operations  14.6 us (2%)
    all_gather x6, waiting for transfers between devices, entering(): gathered = jax.tree.map(lambda a: lax.all_gather(a, axis), part)  317 us
    psum x2, waiting for transfers between devices, produce_ticks_on(): m = lax.psum(m, axis_name=h)  108 us
    psum x1, waiting for transfers between devices, run_chain(): group_sum = lax.psum((local_terms[0], local_terms[1]), 'sc')  93.1 us
    psum x1, waiting for transfers between devices, run_chain(): block_sum = lax.psum((group_sum[0], group_sum[1]), 'sb')  29.4 us
    dot_general x1, matrix products, shards(): jnp.einsum('hts,shd->thd', grad_scores, key_t, precision=highest)  21 us
    dot_general x1, matrix products, shards(): jnp.einsum('thd,shd->hts', query_t, key_t, precision=highest) * lower  19.5 us
    unnamed x22, local copies, waits for them, and re-layouts  19 us
    dot_general x1, matrix products, shards(): jnp.einsum('hts,thd->shd', grad_scores, query_t, precision=highest)  14.8 us
  transfers between devices with their start and end apart: 10, of which 9 were waited for; matrix products, arithmetic and copies ran while one was open for 13% of the time, Pallas kernels for 0%

profile of v1, /device:TPU:1, one launch (start us, length us, event | category | flops | bytes accessed | tf_op | source)
XLA Modules:
  0.0 724.6 jit_solution(9599324191952776128)
XLA Ops:
  7.2 11.2 %fusion.21 = f32[16,128,128]{2,1,0:T(8,128)} fusion(f32[512,2048]{1,0:T(8,128)} %param.14, f32[512,2048]{1,0:T(8,128)} %param.13), kind=kOutput, calls=%fused_computation.27 | convolution fusion | flops 1610612736 | bytes 9437184 | tf_op jit(solution)/shard_map/thd,the->hde/dot_general | solution.py:53
  18.4 5.1 copy.46
  23.5 5.7 copy.27
  29.2 9.2 %fusion.16 = f32[16,128,128]{2,1,0:T(8,128)} fusion(f32[512,16,128]{0,2,1:T(8,128)} %copy.27, f32[512,2048]{1,0:T(8,128)} %param.12), kind=kOutput, calls=%fused_computation.22 | convolution fusion | flops 1610612736 | bytes 9437184 | tf_op jit(solution)/shard_map/the,thd->hed/dot_general | solution.py:54
  38.4 94.8 %all-gather.19.cloned.1.call-done = f32[256,128,128]{2,1,0:T(8,128)} async-done(((f32[16,128,128]{2,1,0:T(8,128)}), f32[256,128,128]{2,1,0:T(8,128)}) %all-gather.19.cloned.1.call-update) | async-done | bytes 16777232 | tf_op jit(solution)/shard_map/all_gather | solution.py:16
  133.2 0.7 all-reduce.11.cloned.1.call-update
  134.0 93.1 %all-reduce.11.cloned.1.call-done = (f32[16,128,128]{2,1,0:T(8,128)}, f32[16,128,128]{2,1,0:T(8,128)}) async-done(((f32[16,128,128]{2,1,0:T(8,128)}, f32[16,128,128]{2,1,0:T(8,128)}), (f32[16,128,128]{2,1,0:T(8,128)}, f32[16,128,128]{2,1,0:T(8,128)})) %all-reduce.11.cloned.1.call-update) | async-done | bytes 2097168 | tf_op jit(solution)/shard_map/psum | solution.py:34
  227.7 15.4 %all-gather.15.cloned.1.call-done = f32[32,128,128]{2,1,0:T(8,128)} async-done(((f32[16,128,128]{2,1,0:T(8,128)}), f32[32,128,128]{2,1,0:T(8,128)}) %all-gather.15.cloned.1.call-update) | async-done | bytes 2097168 | tf_op jit(solution)/shard_map/all_gather | solution.py:16
  243.1 16.3 %all-gather.17.cloned.1.call-done = f32[32,128,128]{2,1,0:T(8,128)} async-done(((f32[16,128,128]{2,1,0:T(8,128)}), f32[32,128,128]{2,1,0:T(8,128)}) %all-gather.17.cloned.1.call-update) | async-done | bytes 2097168 | tf_op jit(solution)/shard_map/all_gather | solution.py:16
  260.6 0.7 all-gather.21.cloned.1.call-update
  261.3 29.4 %all-reduce.13.cloned.1.call-done = (f32[1,16,128,128]{3,2,1,0:T(8,128)}, f32[1,16,128,128]{3,2,1,0:T(8,128)}) async-done(((f32[1,16,128,128]{3,2,1,0:T(8,128)}, f32[1,16,128,128]{3,2,1,0:T(8,128)}), (f32[1,16,128,128]{3,2,1,0:T(8,128)}, f32[1,16,128,128]{3,2,1,0:T(8,128)})) %all-reduce.13.cloned.1.call-update) | async-done | bytes 2097168 | tf_op jit(solution)/shard_map/psum | solution.py:36
  291.7 19.5 %fusion.14 = f32[16,512,512]{2,1,0:T(8,128)} fusion(f32[512,2048]{1,0:T(8,128)} %param.12, f32[512,2048]{1,0:T(8,128)} %param.13), kind=kOutput, calls=%fused_computation.20 | convolution fusion | flops 6442450944 | bytes 25165824 | tf_op jit(solution)/shard_map/thd,shd->hts/dot_general | solution.py:64
  311.3 14.5 %fusion.11 = f32[16,512,512]{2,1,0:T(8,128)S(1)} fusion(f32[512,2048]{1,0:T(8,128)S(1)} %copy-done.4, f32[512,2048]{1,0:T(8,128)S(1)} %copy-done.5), kind=kOutput, calls=%fused_computation.17 | convolution fusion | flops 6442450944 | bytes 25165824 | tf_op jit(solution)/shard_map/the,she->hts/dot_general | solution.py:63
  325.7 21.0 %fusion.4 = f32[16,512,128]{1,2,0:T(8,128)} fusion(f32[16,512,512]{2,1,0:T(8,128)S(1)} %fusion.11, f32[512,512]{1,0:T(8,128)S(1)} %fusion.55, f32[512,2048]{1,0:T(8,128)} %param.13), kind=kOutput, calls=%fused_computation.10 | convolution fusion | flops 6446645248 | bytes 26214400 | tf_op jit(solution)/shard_map/hts,shd->thd/dot_general | solution.py:67
  346.7 14.8 %fusion.2 = f32[16,512,128]{1,2,0:T(8,128)} fusion(f32[16,512,512]{2,1,0:T(8,128)S(1)} %fusion.11, f32[512,512]{1,0:T(8,128)S(1)} %fusion.55, f32[512,2048]{1,0:T(8,128)} %param.12), kind=kOutput, calls=%fused_computation.8 | convolution fusion | flops 6446645248 | bytes 26214400 | tf_op jit(solution)/shard_map/hts,thd->shd/dot_general | solution.py:71
  361.6 93.9 %all-gather.21.cloned.1.call-done = f32[256,128,128]{2,1,0:T(8,128)} async-done(((f32[16,128,128]{2,1,0:T(8,128)}), f32[256,128,128]{2,1,0:T(8,128)}) %all-gather.21.cloned.1.call-update) | async-done | bytes 16777232 | tf_op jit(solution)/shard_map/all_gather | solution.py:16
  455.7 1.0 copy-done.1
  456.9 2.1 while.37
  456.9 2.1 bitcast_add_fusion.13
  459.0 46.1 %all-gather.11.cloned.1.call-done = f32[4,16,128,128]{3,2,1,0:T(8,128)} async-done(((f32[1,16,128,128]{3,2,1,0:T(8,128)}), f32[4,16,128,128]{3,2,1,0:T(8,128)}) %all-gather.11.cloned.1.call-update) | async-done | bytes 4194320 | tf_op jit(solution)/shard_map/all_gather | solution.py:16
  505.1 50.4 %all-gather.13.cloned.1.call-done = f32[4,16,128,128]{3,2,1,0:T(8,128)} async-done(((f32[1,16,128,128]{3,2,1,0:T(8,128)}), f32[4,16,128,128]{3,2,1,0:T(8,128)}) %all-gather.13.cloned.1.call-update) | async-done | bytes 4194320 | tf_op jit(solution)/shard_map/all_gather | solution.py:16
  555.6 1.1 broadcast.6.clone.3
  556.7 107.6 %all-reduce.9.cloned.1.call-done = f32[16,128,128]{2,1,0:T(8,128)} async-done(((f32[16,128,128]{2,1,0:T(8,128)}), f32[16,128,128]{2,1,0:T(8,128)}) %all-reduce.9.cloned.1.call-update) | async-done | bytes 1048592 | tf_op jit(solution)/shard_map/psum | solution.py:10
  664.3 3.5 subtract_add_fusion
  667.8 1.0 copy-done.8
  668.8 3.8 fusion.23
  672.6 14.6 %fusion.29 = bf16[512,16,128]{0,2,1:T(8,128)(2,1)} fusion(f32[16,128,512]{2,1,0:T(8,128)S(1)} %fusion.23, f32[512,16,128]{0,2,1:T(8,128)S(1)} %copy-done.3, f32[16,512,512]{2,1,0:T(8,128)} %fusion.14, f32[512,512]{1,0:T(8,128)S(1)} %copy-done.7), kind=kOutput, calls=%fused_computation.36 | convolution fusion | flops 6449790976 | bytes 28311552 | tf_op jit(solution)/shard_map/hts,the->she/dot_general | solution.py:75
  687.2 3.9 copy.40
  691.2 9.2 %fusion.31 = bf16[512,16,128]{0,2,1:T(8,128)(2,1)} fusion(f32[16,512,128]{1,2,0:T(8,128)} %fusion.2, f32[16,128,128]{2,1,0:T(8,128)} %copy-done.8, f32[512,2048]{1,0:T(8,128)} %param.14), kind=kOutput, calls=%fused_computation.39 | convolution fusion | flops 1613758464 | bytes 11534336 | tf_op jit(solution)/shard_map/she,hed->shd/dot_general | solution.py:70
  700.3 4.1 copy.39
  704.4 9.2 %fusion.33 = bf16[512,16,128]{0,2,1:T(8,128)(2,1)} fusion(f32[16,512,128]{1,2,0:T(8,128)} %fusion.4, f32[16,128,128]{2,1,0:T(8,128)} %param.16, f32[16,128,128]{2,1,0:T(8,128)S(1)} %get-tuple-element.107, f32[16,128,128]{2,1,0:T(8,128)S(1)} %get-tuple-element.105, f32[16,128,128]{2,1,0:T(8,128)S(1)} %get-tuple-element.106, f32[512,2048]{1,0:T(8,128)} %param.15), kind=kOutput, calls=%fused_computation.42 | convolution fusion | flops 1614544896 | bytes 14680064 | tf_op jit(solution)/shard_map/the,hde->thd/dot_general | solution.py:66
  713.6 3.9 copy.38
  (43 shorter events, 3.3 us)
Async XLA Ops:
  7.2 126.0 %all-gather.19.cloned.1.call-start = ((), (), s32[]{:S(2)}) async-start(), calls=%async_computation.6 | async-start | bytes 17825792 | tf_op jit(solution)/shard_map/all_gather | solution.py:16
  133.2 93.9 %all-reduce.11.cloned.1.call-start = ((), (), s32[]{:S(2)}) async-start(), calls=%async_computation.8 | async-start | bytes 4194304 | tf_op jit(solution)/shard_map/psum | solution.py:34
  133.9 109.2 %all-gather.15.cloned.1.call-start = ((), (), s32[]{:S(2)}) async-start(), calls=%async_computation.4 | async-start | bytes 3145728 | tf_op jit(solution)/shard_map/all_gather | solution.py:16
  227.1 32.2 %all-gather.17.cloned.1.call-start = ((), (), s32[]{:S(2)}) async-start(), calls=%async_computation.5 | async-start | bytes 3145728 | tf_op jit(solution)/shard_map/all_gather | solution.py:16
  259.4 31.4 %all-reduce.13.cloned.1.call-start = ((), (), s32[]{:S(2)}) async-start(), calls=%async_computation.9 | async-start | bytes 4194304 | tf_op jit(solution)/shard_map/psum | solution.py:36
  259.9 101.6 %all-reduce.7.cloned.1.call-start = ((), (), s32[]{:S(2)}) async-start(), calls=%async_computation.2 | async-start | bytes 2097152 | tf_op jit(solution)/shard_map/psum | solution.py:10
  260.5 195.0 %all-gather.21.cloned.1.call-start = ((), (), s32[]{:S(2)}) async-start(), calls=%async_computation.7 | async-start | bytes 17825792 | tf_op jit(solution)/shard_map/all_gather | solution.py:16
  261.3 243.9 %all-gather.11.cloned.1.call-start = ((), (), s32[]{:S(2)}) async-start(), calls=%async_computation | async-start | bytes 5242880 | tf_op jit(solution)/shard_map/all_gather | solution.py:16
  290.8 264.8 %all-gather.13.cloned.1.call-start = ((), (), s32[]{:S(2)}) async-start(), calls=%async_computation.1 | async-start | bytes 5242880 | tf_op jit(solution)/shard_map/all_gather | solution.py:16
  291.5 372.8 %all-reduce.9.cloned.1.call-start = ((), (), s32[]{:S(2)}) async-start(), calls=%async_computation.3 | async-start | bytes 2097152 | tf_op jit(solution)/shard_map/psum | solution.py:10
  291.7 55.0 %copy-start.6 = (f32[512,512]{1,0:T(8,128)}, f32[512,512]{1,0:T(8,128)S(1)}, u32[]{:S(2)}) copy-start(f32[512,512]{1,0:T(8,128)S(1)} %fusion.55) | copy-start | bytes 3145732
  291.7 19.6 %copy-start.4 = (f32[512,2048]{1,0:T(8,128)S(1)}, f32[512,2048]{1,0:T(8,128)}, u32[]{:S(2)}) copy-start(f32[512,2048]{1,0:T(8,128)} %param.15) | copy-start | bytes 12582916
  291.7 19.6 %copy-start.5 = (f32[512,2048]{1,0:T(8,128)S(1)}, f32[512,2048]{1,0:T(8,128)}, u32[]{:S(2)}) copy-start(f32[512,2048]{1,0:T(8,128)} %param.14) | copy-start | bytes 12582916
  455.7 1.0 copy-start.1
  459.0 46.1 %copy-start.2 = (f32[16,128,128]{2,1,0:T(8,128)}, f32[16,128,128]{2,1,0:T(8,128)S(1)}, u32[]{:S(2)}) copy-start(f32[16,128,128]{2,1,0:T(8,128)S(1)} %get-tuple-element.109) | copy-start | bytes 3145732
  664.3 4.5 copy-start
  667.8 1.0 copy-start.8
  668.8 3.8 copy-start.3
  668.8 3.8 copy-start.7
Sparse Core Ops, SparseCore 0:
  18.5 114.6 all-gather.18
  138.0 89.0 all-reduce.10
  228.9 14.2 all-gather.14
  244.7 14.6 all-gather.16
  262.5 28.1 all-reduce.12
  293.5 45.2 all-reduce.6
  341.8 113.6 all-gather.20
  457.3 47.8 all-gather.10
  506.9 48.5 all-gather.12
  559.0 105.2 all-reduce.8
